TPU v7x, 32 devices: a whole 2x2x4 slice. The times are simulated.
32 devices in a mesh: tm: 16 (over z, x, core), space: 2 (over y).
Axes of the slice: x: 2, y: 2, z: 4, core: 2. Of those that a mesh axis runs over, the one named last changes fastest.
Arguments:
- nodes: float32 [16, 2, 2, 8, 128, 128], P('tm', None, None, 'space'), may hold values from -3 to 3
- initial: float32 [2, 8, 128, 128], P(None, 'space'), may hold values from -3 to 3
Outputs:
- corrected: float32 [16, 2, 2, 8, 128, 128], P('tm', None, None, 'space')
All inputs are finite; a program needn't handle non-finite values.
Results may differ from a plain program's by a relative error of at most 0.0003.
Values sent between devices are 32-bit elements; how exact they have to be, the bound alone decides.
No kernel may reach another device: no remote copies, remote signals or barrier semaphores. Data moves between devices by JAX's collectives and lax.ppermute only.
A program may use at most 128 MiB of HBM per device.

v0:
```python
import math
import jax
import jax.numpy as jnp
from jax import lax
from jax.sharding import PartitionSpec as P

diffuse_fast = 0.5
diffuse_slow = 0.25
feed_rate = 0.04
kill_rate = 0.06
slice_length = 0.5
node_step = 0.25
sweep_weights = ((5.0 / 24.0, 1.0 / 3.0, -1.0 / 24.0), (-1.0 / 24.0, 1.0 / 3.0, 5.0 / 24.0))


def with_halo(x, sides, width):
    for axis, dim in sides:
        devices, length = (lax.axis_size(axis), x.shape[dim])
        up = [(i, (i + 1) % devices) for i in range(devices - 1)]
        down = [(j, i) for i, j in up]
        last = lax.slice_in_dim(x, length - width, length, axis=dim)
        leading = lax.slice_in_dim(x, 0, width, axis=dim)
        before = lax.ppermute(last, axis, up)
        after = lax.ppermute(leading, axis, down)
        x = jnp.concatenate([before, x, after], axis=dim)
    return x


def passed_along(value, axis, steps):
    count = lax.axis_size(axis)
    leading, last = (max(0, -steps), min(count, count - steps))
    return lax.ppermute(value, axis, [(source, source + steps) for source in range(leading, last)])


def entering(value, axis, join, neutral):
    count, mine = (lax.axis_size(axis), lax.axis_index(axis))
    pieces = jax.tree.map(lambda part: lax.all_gather(part, axis), value)
    subtotal = jax.tree.map(
        lambda part, zero: jnp.full_like(part, 0) + jnp.asarray(zero, part.dtype), value, neutral
    )

    def lap(position, subtotal):
        longer = join(subtotal, jax.tree.map(lambda part: part[position], pieces))
        return jax.tree.map(lambda new, old: jnp.where(position < mine, new, old), longer, subtotal)

    return lax.fori_loop(0, count - 1, lap, subtotal)


def sine_table(points, modes, stretch):
    place = jnp.arange(points).astype(jnp.float32) + 0.5
    order = jnp.arange(modes).astype(jnp.float32) + 1.0
    angle = math.pi / (stretch * modes) * place[:, None] * order[None, :]
    weight = jnp.where(jnp.arange(modes) == modes - 1, math.sqrt(0.5), 1.0).astype(jnp.float32)
    return math.sqrt(2.0 / modes) * weight[None, :] * jnp.sin(angle)


def tendency(values):
    center = values[..., 1:-1, :, :]
    padded = jnp.pad(center, [(0, 0)] * (center.ndim - 2) + [(1, 1), (1, 1)])
    laplace = (
        values[..., 2:, :, :]
        + values[..., :-2, :, :]
        + padded[..., 2:, 1:-1]
        + padded[..., :-2, 1:-1]
    )
    laplace = laplace + padded[..., 1:-1, 2:] + padded[..., 1:-1, :-2] - 6.0 * center
    first_kind = center[..., 0, :, :, :]
    second_kind = center[..., 1, :, :, :]
    reaction = (1.0 + first_kind) * second_kind * second_kind
    first_rate = diffuse_fast * laplace[..., 0, :, :, :] - reaction - feed_rate * first_kind
    second_rate = (
        diffuse_slow * laplace[..., 1, :, :, :] + reaction - (feed_rate + kill_rate) * second_kind
    )
    return jnp.stack([first_rate, second_rate], axis=-4)


def restrict(values):
    shape = values.shape
    blocks = values.reshape(shape[:-3] + (shape[-3] // 2, 2, shape[-2] // 2, 2, shape[-1] // 2, 2))
    return jnp.mean(blocks, axis=(-5, -3, -1))


def with_rims(values):
    return with_halo(values, (("space", 2),), 1)


def local(nodes, initial):
    planes_dev = initial.shape[1]
    width_x = initial.shape[2]
    width_y = initial.shape[3]
    spaces = lax.axis_size("space")
    modes_x = width_x // 2
    modes_y = width_y // 2
    modes_z = planes_dev * spaces // 2
    columns = modes_x * modes_y // spaces
    highest = lax.Precision.HIGHEST
    (w00, w01, w02), (w10, w11, w12) = sweep_weights
    own_nodes = nodes[0]
    prior_end = passed_along(own_nodes[1], "tm", 1)
    is_first = lax.axis_index("tm") == 0
    start_value = jnp.where(is_first, initial, prior_end)
    stacked = jnp.stack([start_value, own_nodes[0], own_nodes[1]])
    slopes = tendency(with_rims(stacked))
    swept_one = start_value + slice_length * (w00 * slopes[0] + w01 * slopes[1] + w02 * slopes[2])
    slope_one = tendency(with_rims(swept_one[None]))[0]
    swept_two = (
        swept_one
        + node_step * (slope_one - slopes[1])
        + slice_length * (w10 * slopes[0] + w11 * slopes[1] + w12 * slopes[2])
    )
    slope_two = tendency(with_rims(swept_two[None]))[0]
    integral_one = slice_length * (w00 * slopes[0] + w01 * slope_one + w02 * slope_two)
    integral_two = slice_length * (w10 * slopes[0] + w11 * slope_one + w12 * slope_two)
    coarse = restrict(jnp.stack([integral_one, integral_two, start_value, swept_one, swept_two]))
    forward_x = sine_table(modes_x, modes_x, 1.0).T
    forward_y = sine_table(modes_y, modes_y, 1.0).T
    forward_z = sine_table(modes_z, modes_z, 1.0).T
    along_y = jnp.einsum("by,fszxy->fszxb", forward_y, coarse, precision=highest)
    spectra_xy = jnp.einsum("ax,fszxb->fszab", forward_x, along_y, precision=highest)
    spectra_xy = spectra_xy.reshape(5, 2, planes_dev // 2, modes_x * modes_y)
    gathered = lax.all_to_all(spectra_xy, "space", split_axis=3, concat_axis=2, tiled=True)
    spectra = jnp.einsum("kz,fszc->fskc", forward_z, gathered, precision=highest)
    column_ids = lax.axis_index("space") * columns + jnp.arange(columns)
    order_x = (column_ids // modes_y + 1).astype(jnp.float32)
    order_y = (column_ids % modes_y + 1).astype(jnp.float32)
    order_z = jnp.arange(modes_z).astype(jnp.float32) + 1.0
    eigen_xy = (
        2.0 * jnp.cos(math.pi * order_x / modes_x)
        - 2.0
        + 2.0 * jnp.cos(math.pi * order_y / modes_y)
        - 2.0
    )
    eigen_z = 2.0 * jnp.cos(math.pi * order_z / modes_z) - 2.0
    eigen_sum = (eigen_z[:, None] + eigen_xy[None, :]) / 4.0
    linear = jnp.stack(
        [diffuse_fast * eigen_sum - feed_rate, diffuse_slow * eigen_sum - (feed_rate + kill_rate)]
    )
    factor = 1.0 / (1.0 - node_step * linear)
    remain_one = spectra[0] - node_step * linear * spectra[3]
    remain_two = spectra[1] - node_step * linear * spectra[4]
    seed_value = jnp.where(is_first, spectra[2], 0.0)
    element = factor * (factor * (seed_value + remain_one) + remain_two)
    log_gain = 2.0 * jnp.log(factor)

    def join_counts(earlier, later):
        return (earlier[0] + later[0], jnp.exp(later[0] * log_gain) * earlier[1] + later[1])

    _, prefix = entering(
        (jnp.ones((), jnp.float32), element),
        "tm",
        join_counts,
        (jnp.zeros((), jnp.float32), jnp.zeros_like(element)),
    )
    start_hat = jnp.where(is_first, spectra[2], prefix)
    new_one = factor * (start_hat + remain_one)
    new_two = factor * (new_one + remain_two)
    change = jnp.stack([new_one - spectra[3], new_two - spectra[4]])
    interp_x = sine_table(width_x, modes_x, 2.0)
    interp_y = sine_table(width_y, modes_y, 2.0)
    interp_z = sine_table(planes_dev * spaces, modes_z, 2.0)
    at_planes = jnp.einsum("zk,fskc->fszc", interp_z, change, precision=highest)
    returned = lax.all_to_all(at_planes, "space", split_axis=2, concat_axis=3, tiled=True)
    returned = returned.reshape(2, 2, planes_dev, modes_x, modes_y)
    widened_y = jnp.einsum("yb,fszab->fszay", interp_y, returned, precision=highest)
    refined = jnp.einsum("xa,fszay->fszxy", interp_x, widened_y, precision=highest)
    corrected = jnp.stack([swept_one + refined[0], swept_two + refined[1]])
    return corrected[None]


def solution(mesh):
    in_specs = (P("tm", None, None, "space", None, None), P(None, "space", None, None))
    out_specs = P("tm", None, None, "space", None, None)
    return jax.shard_map(local, mesh=mesh, in_specs=in_specs, out_specs=out_specs, check_vma=False)
```

profile of v0, /device:TPU:0, one launch (start us, length us, event | category | flops | bytes accessed | tf_op | source)
XLA Modules:
  0.0 521.1 jit_solution(6361830666859375832)
XLA Ops:
  14.4 6.0 %collective-permute-start.2 = (f32[3,2,1,128,128]{3,4,2,1,0:T(8,128)S(1)}, f32[3,2,1,128,128]{3,4,2,1,0:T(8,128)}, u32[]{:S(2)}, u32[]{:S(2)}) collective-permute-start(f32[3,2,1,128,128]{3,4,2,1,0:T(8,128)S(1)} %get-tuple-element.157), channel_id=1, source_target_pairs={{0,1},{2,3},{4,5},{6,7},{8,9},{10,11},{12,13},{14,15},{16,17},{18,... | collective-permute-start | bytes 1179656 | tf_op jit(solution)/shard_map/ppermute | solution.py:23
  28.9 4.6 collective-permute-start.4
  38.6 4.8 collective-permute-start.6
  43.5 34.9 %reshape.454 = f32[1,2,2,2,64,2,64,2]{5,4,7,6,3,2,1,0:T(8,128)} reshape(f32[2,4,128,128]{2,3,1,0:T(8,128)S(1)} %broadcast_select_fusion) | data formatting | bytes 1048576 | tf_op jit(solution)/shard_map/stack | solution.py:114
  78.4 22.8 %copy.49 = f32[1,2,2,2,64,2,64,2]{6,4,7,5,3,2,1,0:T(8,128)S(1)} copy(f32[1,2,2,2,64,2,64,2]{5,4,7,6,3,2,1,0:T(8,128)} %reshape.454) | data formatting | bytes 1048576 | tf_op jit(solution)/shard_map/stack | solution.py:114
  101.2 34.8 %reshape.455 = f32[1,2,2,2,64,2,64,2]{5,4,7,6,3,2,1,0:T(8,128)} reshape(f32[2,4,128,128]{2,3,1,0:T(8,128)S(1)} %get-tuple-element.150) | data formatting | bytes 1048576 | tf_op jit(solution)/shard_map/stack | solution.py:114
  136.0 23.8 %copy.50 = f32[1,2,2,2,64,2,64,2]{6,4,7,5,3,2,1,0:T(8,128)} copy(f32[1,2,2,2,64,2,64,2]{5,4,7,6,3,2,1,0:T(8,128)} %reshape.455) | data formatting | bytes 1048576 | tf_op jit(solution)/shard_map/stack | solution.py:114
  159.8 34.8 %reshape.456 = f32[1,2,2,2,64,2,64,2]{5,4,7,6,3,2,1,0:T(8,128)} reshape(f32[2,4,128,128]{2,3,1,0:T(8,128)S(1)} %bitcast_add_fusion.1) | data formatting | bytes 1048576 | tf_op jit(solution)/shard_map/stack | solution.py:114
  194.6 23.8 %copy.51 = f32[1,2,2,2,64,2,64,2]{6,4,7,5,3,2,1,0:T(8,128)} copy(f32[1,2,2,2,64,2,64,2]{5,4,7,6,3,2,1,0:T(8,128)} %reshape.456) | data formatting | bytes 1048576 | tf_op jit(solution)/shard_map/stack | solution.py:114
  220.1 35.6 %reshape.452 = f32[1,2,2,2,64,2,64,2]{5,4,7,6,3,2,1,0:T(8,128)} reshape(f32[1,2,4,128,128]{3,4,2,1,0:T(8,128)} %get-tuple-element.155) | data formatting | bytes 1048576 | tf_op jit(solution)/shard_map/stack | solution.py:114
  255.7 23.8 %copy.47 = f32[1,2,2,2,64,2,64,2]{6,4,7,5,3,2,1,0:T(8,128)} copy(f32[1,2,2,2,64,2,64,2]{5,4,7,6,3,2,1,0:T(8,128)} %reshape.452) | data formatting | bytes 1048576 | tf_op jit(solution)/shard_map/stack | solution.py:114
  281.8 34.8 %reshape.453 = f32[1,2,2,2,64,2,64,2]{5,4,7,6,3,2,1,0:T(8,128)} reshape(f32[1,2,4,128,128]{3,4,2,1,0:T(8,128)S(1)} %copy-done.2) | data formatting | bytes 1048576 | tf_op jit(solution)/shard_map/stack | solution.py:114
  316.7 24.3 %copy.48 = f32[1,2,2,2,64,2,64,2]{6,4,7,5,3,2,1,0:T(8,128)} copy(f32[1,2,2,2,64,2,64,2]{5,4,7,6,3,2,1,0:T(8,128)} %reshape.453) | data formatting | bytes 1048576 | tf_op jit(solution)/shard_map/stack | solution.py:114
  353.8 9.3 %copy.74 = f32[5,2,2,64,64]{0,2,1,4,3:T(2,128)} copy(f32[5,2,2,64,64]{3,4,2,1,0:T(8,128)S(1)} %convolution_bitcast_fusion.3) | data formatting | bytes 655360 | tf_op jit(solution)/shard_map/reshape | solution.py:120
  363.1 15.4 %reshape.457 = f32[2,1,40960]{2,1,0:T(1,128)} reshape(f32[4096,2,2,5]{3,2,1,0:T(2,128)} %bitcast.154) | data formatting | bytes 655360
  378.5 3.5 all-to-all-start
  382.2 5.3 %all-to-all-done = f32[2,1,40960]{2,1,0:T(1,128)S(1)} async-done(((f32[2,1,40960]{2,1,0:T(1,128)}), f32[2,1,40960]{2,1,0:T(1,128)S(1)}, u32[]{:S(2)}, u32[]{:S(2)}) %all-to-all-start) | async-done | bytes 327712 | tf_op jit(solution)/shard_map/all_to_all | solution.py:121
  389.7 15.5 %reshape.458 = f32[4096,2,2,5]{3,2,1,0:T(2,128)} reshape(f32[2,40960]{1,0:T(2,128)S(1)} %reduce) | data formatting | bytes 655360
  405.1 10.3 %copy.55 = f32[5,2,2,2,2048]{4,2,3,1,0:T(2,128)S(1)} copy(f32[5,2,2,2,2048]{0,2,1,4,3:T(2,128)} %bitcast.155) | data formatting | bytes 655360 | tf_op jit(solution)/shard_map/all_to_all | solution.py:121
  418.6 39.5 %all-reduce.3 = f32[16]{0:T(128)S(1)} all-reduce(f32[16]{0:T(128)S(1)} %dynamic-update-slice), channel_id=1, replica_groups=mesh['tm'=16,'space'=2] {'tm'}, use_global_device_ids=true, to_apply=%add.3 | all-reduce | flops 16 | bytes 128
  458.1 7.7 %all-gather.2.cloned.1.call-done = f32[16,2,4,2048]{3,2,1,0:T(4,128)} async-done(((f32[1,2,4,2048]{3,2,1,0:T(4,128)}), f32[16,2,4,2048]{3,2,1,0:T(4,128)}) %all-gather.2.cloned.1.call-update) | async-done | bytes 1048592 | tf_op jit(solution)/shard_map/all_gather | solution.py:37
  465.8 32.5 %while.14 = (s32[]{:T(128)}, f32[2,4,2048]{2,1,0:T(4,128)S(1)}, s32[]{:T(128)}, f32[16]{0:T(128)S(1)}, f32[2,4,2048]{2,1,0:T(4,128)S(1)}, /*index=5*/f32[16,2,4,2048]{3,2,1,0:T(4,128)}, s32[]{:T(128)}, s32[]{:T(128)}) while((s32[]{:T(128)}, f32[2,4,2048]{2,1,0:T(4,128)S(1)}, s32[]{:T(128)}, f32[16]{0:T(128)S(1)}, ...), condition=%wide.region_2.3_spmd.clone, body=%wide.region_1.2_spmd.clone.sunk | while | flops 81924 | bytes 262269 | solution.py:46
  499.9 3.7 all-to-all-start.1
  503.6 5.8 %all-to-all-done.1 = f32[2,2,8,2048]{3,1,0,2:T(2,128)S(1)} async-done(((f32[2,2,8,2048]{3,1,0,2:T(2,128)}), f32[2,2,8,2048]{3,1,0,2:T(2,128)S(1)}, u32[]{:S(2)}, u32[]{:S(2)}) %all-to-all-start.1) | async-done | bytes 262176 | tf_op jit(solution)/shard_map/all_to_all | solution.py:162
  (109 shorter events, 82.4 us)
Async XLA Ops:
  6.5 4.8 copy-start.3
  8.1 4.1 collective-permute-start
  13.2 10.0 %collective-permute-start.1 = (f32[3,2,1,128,128]{3,4,2,1,0:T(8,128)}, f32[3,2,1,128,128]{3,4,2,1,0:T(8,128)}, u32[]{:S(2)}, u32[]{:S(2)}) collective-permute-start(f32[3,2,1,128,128]{3,4,2,1,0:T(8,128)} %get-tuple-element.156), channel_id=1, source_target_pairs={{1,0},{3,2},{5,4},{7,6},{9,8},{11,10},{13,12},{15,14},{17,16},{19,... | collective-permute-start | bytes 1179656 | tf_op jit(solution)/shard_map/ppermute | solution.py:24
  14.4 10.6 %collective-permute-start.2 = (f32[3,2,1,128,128]{3,4,2,1,0:T(8,128)S(1)}, f32[3,2,1,128,128]{3,4,2,1,0:T(8,128)}, u32[]{:S(2)}, u32[]{:S(2)}) collective-permute-start(f32[3,2,1,128,128]{3,4,2,1,0:T(8,128)S(1)} %get-tuple-element.157), channel_id=1, source_target_pairs={{0,1},{2,3},{4,5},{6,7},{8,9},{10,11},{12,13},{14,15},{16,17},{18,... | collective-permute-start | bytes 1179656 | tf_op jit(solution)/shard_map/ppermute | solution.py:23
  27.6 6.9 %collective-permute-start.3 = (f32[1,2,1,128,128]{3,4,2,1,0:T(8,128)S(1)}, f32[1,2,1,128,128]{3,4,2,1,0:T(8,128)S(1)}, u32[]{:S(2)}, u32[]{:S(2)}) collective-permute-start(f32[1,2,1,128,128]{3,4,2,1,0:T(8,128)S(1)} %get-tuple-element.168), channel_id=1, source_target_pairs={{1,0},{3,2},{5,4},{7,6},{9,8},{11,10},{13,12},{15,14},{17,16},{19,... | collective-permute-start | bytes 393224 | tf_op jit(solution)/shard_map/ppermute | solution.py:24
  28.9 7.1 %collective-permute-start.4 = (f32[1,2,1,128,128]{3,4,2,1,0:T(8,128)S(1)}, f32[1,2,1,128,128]{3,4,2,1,0:T(8,128)S(1)}, u32[]{:S(2)}, u32[]{:S(2)}) collective-permute-start(f32[1,2,1,128,128]{3,4,2,1,0:T(8,128)S(1)} %get-tuple-element.169), channel_id=1, source_target_pairs={{0,1},{2,3},{4,5},{6,7},{8,9},{10,11},{12,13},{14,15},{16,17},{18,... | collective-permute-start | bytes 393224 | tf_op jit(solution)/shard_map/ppermute | solution.py:23
  37.3 181.1 %collective-permute-start.5 = (f32[1,2,1,128,128]{3,4,2,1,0:T(8,128)}, f32[1,2,1,128,128]{3,4,2,1,0:T(8,128)S(1)}, u32[]{:S(2)}, u32[]{:S(2)}) collective-permute-start(f32[1,2,1,128,128]{3,4,2,1,0:T(8,128)} %get-tuple-element.166), channel_id=1, source_target_pairs={{1,0},{3,2},{5,4},{7,6},{9,8},{11,10},{13,12},{15,14},{17,16},{19,... | collective-permute-start | bytes 393224 | tf_op jit(solution)/shard_map/ppermute | solution.py:24
  38.6 179.8 %collective-permute-start.6 = (f32[1,2,1,128,128]{3,4,2,1,0:T(8,128)}, f32[1,2,1,128,128]{3,4,2,1,0:T(8,128)S(1)}, u32[]{:S(2)}, u32[]{:S(2)}) collective-permute-start(f32[1,2,1,128,128]{3,4,2,1,0:T(8,128)} %get-tuple-element.167), channel_id=1, source_target_pairs={{0,1},{2,3},{4,5},{6,7},{8,9},{10,11},{12,13},{14,15},{16,17},{18,... | collective-permute-start | bytes 393224 | tf_op jit(solution)/shard_map/ppermute | solution.py:23
  279.4 2.4 copy-start.2
  343.3 1.6 copy-start
  344.9 1.6 copy-start.1
  378.5 9.0 %all-to-all-start = ((f32[2,1,40960]{2,1,0:T(1,128)}), f32[2,1,40960]{2,1,0:T(1,128)S(1)}, u32[]{:S(2)}, u32[]{:S(2)}) async-start(f32[2,1,40960]{2,1,0:T(1,128)} %reshape.457), calls=%async_computation | async-start | bytes 655360 | tf_op jit(solution)/shard_map/all_to_all | solution.py:121
  382.0 83.8 %all-gather.2.cloned.1.call-start = ((), (), s32[]{:S(2)}) async-start(), calls=%async_computation.2 | async-start | bytes 1114112 | tf_op jit(solution)/shard_map/all_gather | solution.py:37
  415.4 1.8 copy-start.4
  499.9 9.5 %all-to-all-start.1 = ((f32[2,2,8,2048]{3,1,0,2:T(2,128)}), f32[2,2,8,2048]{3,1,0,2:T(2,128)S(1)}, u32[]{:S(2)}, u32[]{:S(2)}) async-start(f32[2,2,8,2048]{3,1,0,2:T(2,128)} %copy.56), calls=%async_computation.1 | async-start | bytes 524288 | tf_op jit(solution)/shard_map/all_to_all | solution.py:162
Sparse Core Ops, SparseCore 0:
  417.4 48.3 all-gather.1
where the time goes:
time: 528 us; the launch traced here: 521 us
  local copies, waits for them, and re-layouts  370 us (70%)
  blocking collectives  39.5 us (7%)
  other arithmetic  34.8 us (7%)
  starting transfers between devices  29.8 us (6%)
  waiting for transfers between devices  26 us (5%)
  between operations  14 us (3%)
  matrix products  6.93 us (1%)
    another operation x11, local copies, waits for them, and re-layouts, local(): jnp.stack([integral_one, integral_two, start_value, swept_one, swept_two])  295 us
    unnamed x22, local copies, waits for them, and re-layouts  40.7 us
    unnamed x1, blocking collectives  39.5 us
    select_n x15, other arithmetic, lap(): jnp.where(position < mine, new, old)  23.6 us
    ppermute x3, starting transfers between devices, with_halo(): before = lax.ppermute(last, axis, up)  15.4 us
    all_to_all x3, local copies, waits for them, and re-layouts, local(): lax.all_to_all(spectra_xy, 'space', split_axis=3, concat_axis=2, tiled=True)  11.1 us
  transfers between devices with their start and end apart: 10, of which 8 were waited for; matrix products, arithmetic and copies ran while one was open for 34% of the time, Pallas kernels for 0%

commit v1 on v0

--- a/solution.py
+++ b/solution.py
@@ -118,7 +118,9 @@
     along_y = jnp.einsum("by,fszxy->fszxb", forward_y, coarse, precision=highest)
     spectra_xy = jnp.einsum("ax,fszxb->fszab", forward_x, along_y, precision=highest)
     spectra_xy = spectra_xy.reshape(5, 2, planes_dev // 2, modes_x * modes_y)
-    gathered = lax.all_to_all(spectra_xy, "space", split_axis=3, concat_axis=2, tiled=True)
+    w2 = jnp.split(spectra_xy, lax.axis_size("space"), axis=3)
+    reply = lax.all_to_all(jnp.stack(w2), axis_name="space", split_axis=0, concat_axis=0)
+    gathered = jnp.concatenate(reply, axis=2)
     spectra = jnp.einsum("kz,fszc->fskc", forward_z, gathered, precision=highest)
     column_ids = lax.axis_index("space") * columns + jnp.arange(columns)
     order_x = (column_ids // modes_y + 1).astype(jnp.float32)

time: 528 us -> 472 us (0.89)
  local copies, waits for them, and re-layouts: 370 us -> 319 us
    unnamed x22 -> x20, local copies, waits for them, and re-layouts: 40.7 us -> 9.74 us
    all_to_all x3 -> x0, local copies, waits for them, and re-layouts: 11.1 us -> none  [local(): lax.all_to_all(spectra_xy, 'space', split_axis=3, concat_axis=2, tiled=True)]
    reshape x1, local copies, waits for them, and re-layouts: 9.27 us -> 0.34 us  [local(): spectra_xy = spectra_xy.reshape(5, 2, planes_dev // 2, modes_x * modes_y)]
  transfers between devices with their start and end apart: 10 -> 10, of which waited for: 8 -> 8; matrix products, arithmetic and copies ran while one was open for 34% -> 38% of each run, Pallas kernels for 0% -> 0%
where the time goes in v1:
time: 472 us; the launch traced here: 469 us
  local copies, waits for them, and re-layouts  319 us (68%)
  blocking collectives  39.5 us (8%)
  other arithmetic  34 us (7%)
  starting transfers between devices  29.5 us (6%)
  waiting for transfers between devices  26.2 us (6%)
  between operations  13.7 us (3%)
  matrix products  6.93 us (1%)
    another operation x11, local copies, waits for them, and re-layouts, local(): jnp.stack([integral_one, integral_two, start_value, swept_one, swept_two])  294 us
    unnamed x1, blocking collectives  39.5 us
    select_n x15, other arithmetic, lap(): jnp.where(position < mine, new, old)  23.6 us
    ppermute x3, starting transfers between devices, with_halo(): before = lax.ppermute(last, axis, up)  15.3 us
    unnamed x20, local copies, waits for them, and re-layouts  9.74 us
  transfers between devices with their start and end apart: 10, of which 8 were waited for; matrix products, arithmetic and copies ran while one was open for 38% of the time, Pallas kernels for 0%

profile of v1, /device:TPU:0, one launch (start us, length us, event | category | flops | bytes accessed | tf_op | source)
XLA Modules:
  0.0 469.1 jit_solution(58851464985563142)
XLA Ops:
  8.1 3.2 collective-permute-start
  14.4 6.0 %collective-permute-start.2 = (f32[3,2,1,128,128]{3,4,2,1,0:T(8,128)S(1)}, f32[3,2,1,128,128]{3,4,2,1,0:T(8,128)}, u32[]{:S(2)}, u32[]{:S(2)}) collective-permute-start(f32[3,2,1,128,128]{3,4,2,1,0:T(8,128)S(1)} %get-tuple-element.157), channel_id=1, source_target_pairs={{0,1},{2,3},{4,5},{6,7},{8,9},{10,11},{12,13},{14,15},{16,17},{18,... | collective-permute-start | bytes 1179656 | tf_op jit(solution)/shard_map/ppermute | solution.py:23
  20.6 2.5 collective-permute-done.1
  28.9 4.6 collective-permute-start.4
  38.7 4.7 %collective-permute-start.6 = (f32[1,2,1,128,128]{3,4,2,1,0:T(8,128)}, f32[1,2,1,128,128]{3,4,2,1,0:T(8,128)S(1)}, u32[]{:S(2)}, u32[]{:S(2)}) collective-permute-start(f32[1,2,1,128,128]{3,4,2,1,0:T(8,128)} %get-tuple-element.167), channel_id=1, source_target_pairs={{0,1},{2,3},{4,5},{6,7},{8,9},{10,11},{12,13},{14,15},{16,17},{18,... | collective-permute-start | bytes 393224 | tf_op jit(solution)/shard_map/ppermute | solution.py:23
  43.4 34.9 %reshape.462 = f32[1,2,2,2,64,2,64,2]{5,4,7,6,3,2,1,0:T(8,128)} reshape(f32[2,4,128,128]{2,3,1,0:T(8,128)S(1)} %broadcast_select_fusion) | data formatting | bytes 1048576 | tf_op jit(solution)/shard_map/stack | solution.py:114
  78.3 22.8 %copy.30 = f32[1,2,2,2,64,2,64,2]{6,4,7,5,3,2,1,0:T(8,128)S(1)} copy(f32[1,2,2,2,64,2,64,2]{5,4,7,6,3,2,1,0:T(8,128)} %reshape.462) | data formatting | bytes 1048576 | tf_op jit(solution)/shard_map/stack | solution.py:114
  101.1 34.9 %reshape.463 = f32[1,2,2,2,64,2,64,2]{5,4,7,6,3,2,1,0:T(8,128)} reshape(f32[2,4,128,128]{2,3,1,0:T(8,128)S(1)} %get-tuple-element.150) | data formatting | bytes 1048576 | tf_op jit(solution)/shard_map/stack | solution.py:114
  136.0 23.8 %copy.31 = f32[1,2,2,2,64,2,64,2]{6,4,7,5,3,2,1,0:T(8,128)} copy(f32[1,2,2,2,64,2,64,2]{5,4,7,6,3,2,1,0:T(8,128)} %reshape.463) | data formatting | bytes 1048576 | tf_op jit(solution)/shard_map/stack | solution.py:114
  159.7 34.8 %reshape.464 = f32[1,2,2,2,64,2,64,2]{5,4,7,6,3,2,1,0:T(8,128)} reshape(f32[2,4,128,128]{2,3,1,0:T(8,128)S(1)} %bitcast_add_fusion.1) | data formatting | bytes 1048576 | tf_op jit(solution)/shard_map/stack | solution.py:114
  194.6 23.8 %copy.32 = f32[1,2,2,2,64,2,64,2]{6,4,7,5,3,2,1,0:T(8,128)} copy(f32[1,2,2,2,64,2,64,2]{5,4,7,6,3,2,1,0:T(8,128)} %reshape.464) | data formatting | bytes 1048576 | tf_op jit(solution)/shard_map/stack | solution.py:114
  220.0 35.6 %reshape.460 = f32[1,2,2,2,64,2,64,2]{5,4,7,6,3,2,1,0:T(8,128)} reshape(f32[1,2,4,128,128]{3,4,2,1,0:T(8,128)} %get-tuple-element.155) | data formatting | bytes 1048576 | tf_op jit(solution)/shard_map/stack | solution.py:114
  255.6 23.8 %copy.28 = f32[1,2,2,2,64,2,64,2]{6,4,7,5,3,2,1,0:T(8,128)} copy(f32[1,2,2,2,64,2,64,2]{5,4,7,6,3,2,1,0:T(8,128)} %reshape.460) | data formatting | bytes 1048576 | tf_op jit(solution)/shard_map/stack | solution.py:114
  279.4 2.4 constant_dynamic-update-slice_fusion.4
  281.7 34.8 %reshape.461 = f32[1,2,2,2,64,2,64,2]{5,4,7,6,3,2,1,0:T(8,128)} reshape(f32[1,2,4,128,128]{3,4,2,1,0:T(8,128)S(1)} %copy-done.2) | data formatting | bytes 1048576 | tf_op jit(solution)/shard_map/stack | solution.py:114
  316.6 23.8 %copy.29 = f32[1,2,2,2,64,2,64,2]{6,4,7,5,3,2,1,0:T(8,128)} copy(f32[1,2,2,2,64,2,64,2]{5,4,7,6,3,2,1,0:T(8,128)} %reshape.461) | data formatting | bytes 1048576 | tf_op jit(solution)/shard_map/stack | solution.py:114
  347.0 3.2 reduce_sum.9
  354.7 3.6 all-to-all-start
  358.4 5.4 %all-to-all-done = f32[2,5,2,2,2048]{4,3,2,1,0:T(2,128)S(1)} async-done(((f32[2,5,2,2,2048]{4,3,2,1,0:T(2,128)}), f32[2,5,2,2,2048]{4,3,2,1,0:T(2,128)S(1)}, u32[]{:S(2)}, u32[]{:S(2)}) %all-to-all-start) | async-done | bytes 327712 | tf_op jit(solution)/shard_map/all_to_all | solution.py:122
  366.9 39.5 %all-reduce.3 = f32[16]{0:T(128)S(1)} all-reduce(f32[16]{0:T(128)S(1)} %dynamic-update-slice), channel_id=1, replica_groups=mesh['tm'=16,'space'=2] {'tm'}, use_global_device_ids=true, to_apply=%add.3 | all-reduce | flops 16 | bytes 128
  406.5 7.7 %all-gather.2.cloned.1.call-done = f32[16,2,4,2048]{3,2,1,0:T(4,128)} async-done(((f32[1,2,4,2048]{3,2,1,0:T(4,128)}), f32[16,2,4,2048]{3,2,1,0:T(4,128)}) %all-gather.2.cloned.1.call-update) | async-done | bytes 1048592 | tf_op jit(solution)/shard_map/all_gather | solution.py:37
  414.2 32.5 %while.14 = (s32[]{:T(128)}, f32[2,4,2048]{2,1,0:T(4,128)S(1)}, s32[]{:T(128)}, f32[16]{0:T(128)S(1)}, f32[2,4,2048]{2,1,0:T(4,128)S(1)}, /*index=5*/f32[16,2,4,2048]{3,2,1,0:T(4,128)}, s32[]{:T(128)}, s32[]{:T(128)}) while((s32[]{:T(128)}, f32[2,4,2048]{2,1,0:T(4,128)S(1)}, s32[]{:T(128)}, f32[16]{0:T(128)S(1)}, ...), condition=%wide.region_2.3_spmd.clone, body=%wide.region_1.2_spmd.clone.sunk | while | flops 81924 | bytes 262269 | solution.py:46
  448.3 3.4 all-to-all-start.1
  451.7 5.8 %all-to-all-done.1 = f32[2,2,8,2048]{3,1,0,2:T(2,128)S(1)} async-done(((f32[2,2,8,2048]{3,1,0,2:T(2,128)}), f32[2,2,8,2048]{3,1,0,2:T(2,128)S(1)}, u32[]{:S(2)}, u32[]{:S(2)}) %all-to-all-start.1) | async-done | bytes 262176 | tf_op jit(solution)/shard_map/all_to_all | solution.py:164
  (108 shorter events, 70.2 us)
Async XLA Ops:
  6.5 4.8 %copy-start.3 = (f32[2,4,128,128]{3,2,1,0:T(8,128)S(1)}, f32[2,4,128,128]{3,2,1,0:T(8,128)}, u32[]{:S(2)}) copy-start(f32[2,4,128,128]{3,2,1,0:T(8,128)} %param.5) | copy-start | bytes 1572868
  8.1 4.1 collective-permute-start
  13.2 10.0 %collective-permute-start.1 = (f32[3,2,1,128,128]{3,4,2,1,0:T(8,128)}, f32[3,2,1,128,128]{3,4,2,1,0:T(8,128)}, u32[]{:S(2)}, u32[]{:S(2)}) collective-permute-start(f32[3,2,1,128,128]{3,4,2,1,0:T(8,128)} %get-tuple-element.156), channel_id=1, source_target_pairs={{1,0},{3,2},{5,4},{7,6},{9,8},{11,10},{13,12},{15,14},{17,16},{19,... | collective-permute-start | bytes 1179656 | tf_op jit(solution)/shard_map/ppermute | solution.py:24
  14.4 10.6 %collective-permute-start.2 = (f32[3,2,1,128,128]{3,4,2,1,0:T(8,128)S(1)}, f32[3,2,1,128,128]{3,4,2,1,0:T(8,128)}, u32[]{:S(2)}, u32[]{:S(2)}) collective-permute-start(f32[3,2,1,128,128]{3,4,2,1,0:T(8,128)S(1)} %get-tuple-element.157), channel_id=1, source_target_pairs={{0,1},{2,3},{4,5},{6,7},{8,9},{10,11},{12,13},{14,15},{16,17},{18,... | collective-permute-start | bytes 1179656 | tf_op jit(solution)/shard_map/ppermute | solution.py:23
  27.6 6.9 %collective-permute-start.3 = (f32[1,2,1,128,128]{3,4,2,1,0:T(8,128)S(1)}, f32[1,2,1,128,128]{3,4,2,1,0:T(8,128)S(1)}, u32[]{:S(2)}, u32[]{:S(2)}) collective-permute-start(f32[1,2,1,128,128]{3,4,2,1,0:T(8,128)S(1)} %get-tuple-element.168), channel_id=1, source_target_pairs={{1,0},{3,2},{5,4},{7,6},{9,8},{11,10},{13,12},{15,14},{17,16},{19,... | collective-permute-start | bytes 393224 | tf_op jit(solution)/shard_map/ppermute | solution.py:24
  28.9 7.1 %collective-permute-start.4 = (f32[1,2,1,128,128]{3,4,2,1,0:T(8,128)S(1)}, f32[1,2,1,128,128]{3,4,2,1,0:T(8,128)S(1)}, u32[]{:S(2)}, u32[]{:S(2)}) collective-permute-start(f32[1,2,1,128,128]{3,4,2,1,0:T(8,128)S(1)} %get-tuple-element.169), channel_id=1, source_target_pairs={{0,1},{2,3},{4,5},{6,7},{8,9},{10,11},{12,13},{14,15},{16,17},{18,... | collective-permute-start | bytes 393224 | tf_op jit(solution)/shard_map/ppermute | solution.py:23
  37.4 181.0 %collective-permute-start.5 = (f32[1,2,1,128,128]{3,4,2,1,0:T(8,128)}, f32[1,2,1,128,128]{3,4,2,1,0:T(8,128)S(1)}, u32[]{:S(2)}, u32[]{:S(2)}) collective-permute-start(f32[1,2,1,128,128]{3,4,2,1,0:T(8,128)} %get-tuple-element.166), channel_id=1, source_target_pairs={{1,0},{3,2},{5,4},{7,6},{9,8},{11,10},{13,12},{15,14},{17,16},{19,... | collective-permute-start | bytes 393224 | tf_op jit(solution)/shard_map/ppermute | solution.py:24
  38.7 179.7 %collective-permute-start.6 = (f32[1,2,1,128,128]{3,4,2,1,0:T(8,128)}, f32[1,2,1,128,128]{3,4,2,1,0:T(8,128)S(1)}, u32[]{:S(2)}, u32[]{:S(2)}) collective-permute-start(f32[1,2,1,128,128]{3,4,2,1,0:T(8,128)} %get-tuple-element.167), channel_id=1, source_target_pairs={{0,1},{2,3},{4,5},{6,7},{8,9},{10,11},{12,13},{14,15},{16,17},{18,... | collective-permute-start | bytes 393224 | tf_op jit(solution)/shard_map/ppermute | solution.py:23
  279.4 2.4 copy-start.2
  342.7 1.6 copy-start
  344.3 1.6 copy-start.1
  354.7 10.9 %copy-start.4 = (u32[32]{0:T(128)S(1)}, u32[32]{0:T(128)}, u32[]{:S(2)}) copy-start(u32[32]{0:T(128)} %constant.162) | copy-start | bytes 388
  354.7 9.1 %all-to-all-start = ((f32[2,5,2,2,2048]{4,3,2,1,0:T(2,128)}), f32[2,5,2,2,2048]{4,3,2,1,0:T(2,128)S(1)}, u32[]{:S(2)}, u32[]{:S(2)}) async-start(f32[2,5,2,2,2048]{4,3,2,1,0:T(2,128)} %pad_maximum_fusion.14), calls=%async_computation | async-start | bytes 655360 | tf_op jit(solution)/shard_map/all_to_all | solution.py:122
  358.3 55.9 %all-gather.2.cloned.1.call-start = ((), (), s32[]{:S(2)}) async-start(), calls=%async_computation.2 | async-start | bytes 1114112 | tf_op jit(solution)/shard_map/all_gather | solution.py:37
  448.3 9.3 %all-to-all-start.1 = ((f32[2,2,8,2048]{3,1,0,2:T(2,128)}), f32[2,2,8,2048]{3,1,0,2:T(2,128)S(1)}, u32[]{:S(2)}, u32[]{:S(2)}) async-start(f32[2,2,8,2048]{3,1,0,2:T(2,128)} %copy.36), calls=%async_computation.1 | async-start | bytes 524288 | tf_op jit(solution)/shard_map/all_to_all | solution.py:164
Sparse Core Ops, SparseCore 0:
  365.8 48.3 all-gather.1
